TPU v7x, 32 devices: a whole 2x2x4 slice. The times are simulated.
32 devices in a mesh: rep: 1, ep: 32 (over z, y, x, core).
Axes of the slice: x: 2, y: 2, z: 4, core: 2. Of those that a mesh axis runs over, the one named last changes fastest.
Arguments:
- tokens: bfloat16 [512, 3584], P(('rep', 'ep')), may hold values from -6 to 6
- routes: int32 [512, 8], P(('rep', 'ep')), may hold values from 0 to 15, all different within a row; in each aligned block of 16 rows (0 to 15, 16 to 31, ...) at most 16 rows name the same one
- gate_weights: float32 [512, 8], P(('rep', 'ep')), may hold values from 0.05 to 0.5
- w_gate: bfloat16 [32, 3584, 512], P('ep'), may hold values from -0.09375 to 0.09375
- w_up: bfloat16 [32, 3584, 512], P('ep'), may hold values from -0.09375 to 0.09375
- w_down: bfloat16 [32, 512, 3584], P('ep'), may hold values from -0.1875 to 0.1875
Outputs:
- mixed: bfloat16 [512, 3584], P(('rep', 'ep'))
Inputs may be any that keep to these rules, and one draw needn't show every extreme that they name: `routes`: each token names 8 different experts. Among the tokens of one device at most 16 name any one expert, and in every draw some expert is named by exactly 16 tokens of some device.
All inputs are finite; a program needn't handle non-finite values.
Results may differ from a plain program's by a relative error of at most 0.008.
Values may be sent and summed in bfloat16 or wider, within the bound.
No kernel may reach another device: no remote copies, remote signals or barrier semaphores. Data moves between devices by JAX's collectives and lax.ppermute only.
A program may use at most 128 MiB of HBM per device.

v0:
```python
import jax
import jax.numpy as jnp
from jax import lax
from jax.sharding import PartitionSpec as P


def dense_gates(routes, gate_weights, expert_count):
    hits = routes[:, :, None] == jnp.arange(expert_count, dtype=jnp.int32)[None, None, :]
    return jnp.sum(jnp.where(hits, gate_weights[:, :, None], 0.0), axis=1)


def body(tokens, routes, gate_weights, w_gate, w_up, w_down):
    devices = lax.axis_size("ep")
    expert = lax.axis_index("ep") // 2
    gates = dense_gates(routes, gate_weights, devices // 2)
    all_gates = lax.all_gather(gates, "ep", axis=0, tiled=True)
    rows = lax.all_gather(tokens, "ep", axis=0, tiled=True)
    gate_value = jnp.dot(rows, w_gate[0], preferred_element_type=jnp.float32)
    up_value = jnp.dot(rows, w_up[0], preferred_element_type=jnp.float32)
    hidden = (jax.nn.silu(gate_value) * up_value).astype(jnp.bfloat16)
    partial_value = jnp.dot(hidden, w_down[0], preferred_element_type=jnp.float32)
    mine = jnp.arange(devices // 2, dtype=jnp.int32) == expert
    weight = jnp.sum(jnp.where(mine[None, :], all_gates, 0.0), axis=1)
    weighted = (partial_value * weight[:, None]).astype(jnp.bfloat16)
    return lax.psum_scatter(weighted, "ep", scatter_dimension=0, tiled=True)


def solution(mesh):
    placed = (
        P(("rep", "ep"), None),
        P(("rep", "ep"), None),
        P(("rep", "ep"), None),
        P("ep", None, None),
        P("ep", None, None),
        P("ep", None, None),
    )
    return jax.shard_map(
        body, mesh=mesh, in_specs=placed, out_specs=P(("rep", "ep"), None), check_vma=False
    )
```

profile of v0, /device:TPU:0, one launch (start us, length us, event | category | flops | bytes accessed | tf_op | source)
XLA Modules:
  0.0 235.9 jit_solution(8553971272255911643)
XLA Ops:
  6.5 0.0 all-gather.2.cloned.1.call-start
  6.5 0.7 all-gather.2.cloned.1.call-update
  7.3 0.0 reduce-scatter.2.cloned.1.call-start
  7.3 0.8 copy.9
  8.1 0.8 copy.10
  8.8 0.1 select_reduce_fusion.1
  8.9 44.3 %all_gather.7 = f32[512,16]{1,0:T(8,128)S(1)} all-gather(f32[16,16]{1,0:T(8,128)S(1)} %select_reduce_fusion.1), channel_id=1, replica_groups=mesh['rep'=1,'ep'=32] {'ep'}, dimensions={0}, use_global_device_ids=true | all-gather | bytes 33792 | tf_op jit(solution)/shard_map/all_gather | solution.py:16
  53.2 0.1 select_reduce_fusion
  53.4 20.0 %all-gather.2.cloned.1.call-done = bf16[512,3584]{1,0:T(8,128)(2,1)} async-done(((bf16[16,3584]{1,0:T(8,128)(2,1)}), bf16[512,3584]{1,0:T(8,128)(2,1)}) %all-gather.2.cloned.1.call-update) | async-done | bytes 3670032 | tf_op jit(solution)/shard_map/all_gather | solution.py:17
  73.4 5.2 %fusion.3 = f32[512,512]{1,0:T(8,128)S(1)} fusion(bf16[512,3584]{1,0:T(8,128)(2,1)} %all-gather.2.cloned.1.call-done, bf16[1,3584,512]{2,1,0:T(8,128)(2,1)} %param.9), kind=kOutput, calls=%fused_computation.4 | convolution fusion | flops 1879048192 | bytes 8388608 | tf_op jit(solution)/shard_map/dot_general | solution.py:18
  78.6 10.1 %multiply_convert_fusion = bf16[512,3584]{1,0:T(8,128)(2,1)} fusion(bf16[1,512,3584]{2,1,0:T(8,128)(2,1)} %param.11, f32[512]{0:T(512)S(1)} %select_reduce_fusion, bf16[512,3584]{1,0:T(8,128)(2,1)} %all-gather.2.cloned.1.call-done, bf16[1,3584,512]{2,1,0:T(8,128)(2,1)} %param.10, f32[512,512]{1,0:T(8,128)S(1)} %fusion.3), kind=kOutput, calls=%fused_computation | convolution fusion | flops 3763339264 | bytes 15730688 | tf_op jit(solution)/shard_map/dot_general | solution.py:21
  88.7 0.0 reduce-scatter.2.cloned.1.call-update
  88.7 140.3 %reduce-scatter.2.cloned.1.call-done = bf16[16,3584]{1,0:T(8,128)(2,1)} async-done(((bf16[512,3584]{1,0:T(8,128)(2,1)}), bf16[16,3584]{1,0:T(8,128)(2,1)}) %reduce-scatter.2.cloned.1.call-update) | async-done | bytes 114704 | tf_op jit(solution)/shard_map/reduce_scatter | solution.py:25
  (1 shorter events, 0.0 us)
Async XLA Ops:
  6.5 66.9 %all-gather.2.cloned.1.call-start = ((), (), s32[]{:S(2)}) async-start(), calls=%async_computation.1 | async-start | bytes 3784704 | tf_op jit(solution)/shard_map/all_gather | solution.py:17
  7.3 221.8 %reduce-scatter.2.cloned.1.call-start = ((), (), s32[]{:S(2)}) async-start(), calls=%async_computation.2 | async-start | bytes 3784704 | tf_op jit(solution)/shard_map/reduce_scatter | solution.py:25
Sparse Core Ops, SparseCore 0:
  10.2 63.1 all-gather.1
  88.9 140.1 reduce-scatter.1
where the time goes:
time: 236 us
  waiting for transfers between devices  161 us (68%)
  blocking collectives  44.3 us (19%)
  matrix products  15.3 us (6%)
  between operations  13.4 us (6%)
    reduce_scatter x1, waiting for transfers between devices, body(): return lax.psum_scatter(weighted, 'ep', scatter_dimension=0, tiled=True)  140 us
    all_gather x1, blocking collectives, body(): all_gates = lax.all_gather(gates, 'ep', axis=0, tiled=True)  44.3 us
    all_gather x1, waiting for transfers between devices, body(): rows = lax.all_gather(tokens, 'ep', axis=0, tiled=True)  20 us
    dot_general x1, matrix products, body(): jnp.dot(hidden, w_down[0], preferred_element_type=jnp.float32)  10.1 us
    dot_general x1, matrix products, body(): gate_value = jnp.dot(rows, w_gate[0], preferred_element_type=jnp.float32)  5.21 us
  transfers between devices with their start and end apart: 2, of which 2 were waited for; matrix products, arithmetic and copies ran while one was open for 1% of the time, Pallas kernels for 0%

commit v1 on v0

--- a/solution.py
+++ b/solution.py
@@ -13,8 +13,11 @@
     devices = lax.axis_size("ep")
     expert = lax.axis_index("ep") // 2
     gates = dense_gates(routes, gate_weights, devices // 2)
-    all_gates = lax.all_gather(gates, "ep", axis=0, tiled=True)
-    rows = lax.all_gather(tokens, "ep", axis=0, tiled=True)
+    all_gates, rows = jnp.split(
+        lax.all_gather(jnp.concatenate([gates, tokens], axis=1), "ep", axis=0, tiled=True),
+        [gates.shape[1]],
+        axis=1,
+    )
     gate_value = jnp.dot(rows, w_gate[0], preferred_element_type=jnp.float32)
     up_value = jnp.dot(rows, w_up[0], preferred_element_type=jnp.float32)
     hidden = (jax.nn.silu(gate_value) * up_value).astype(jnp.bfloat16)

time: 236 us -> 253 us (1.072)
  waiting for transfers between devices: 161 us -> 217 us
  blocking collectives: 44.3 us -> 0 us
  other arithmetic: 0.26 us -> 2.94 us
    all_gather x1, waiting for transfers between devices: 20 us -> 76.9 us  [body(): lax.all_gather(jnp.concatenate([gates, tokens], axis=1), 'ep', axis=0, ti...]
    all_gather x1 -> x0, blocking collectives: 44.3 us -> none  [body(): all_gates = lax.all_gather(gates, 'ep', axis=0, tiled=True)]
  transfers between devices with their start and end apart: 2 -> 2, of which waited for: 2 -> 2; matrix products, arithmetic and copies ran while one was open for 1% -> 0% of each run, Pallas kernels for 0% -> 0%
where the time goes in v1:
time: 253 us
  waiting for transfers between devices  217 us (86%)
  matrix products  17.6 us (7%)
  between operations  13.4 us (5%)
  other arithmetic  2.94 us (1%)
    reduce_scatter x1, waiting for transfers between devices, body(): return lax.psum_scatter(weighted, 'ep', scatter_dimension=0, tiled=True)  140 us
    all_gather x1, waiting for transfers between devices, body(): lax.all_gather(jnp.concatenate([gates, tokens], axis=1), 'ep', axis=0, ti...  76.9 us
    dot_general x1, matrix products, body(): jnp.dot(hidden, w_down[0], preferred_element_type=jnp.float32)  11.3 us
    dot_general x1, matrix products, body(): gate_value = jnp.dot(rows, w_gate[0], preferred_element_type=jnp.float32)  6.31 us
  transfers between devices with their start and end apart: 2, of which 2 were waited for; matrix products, arithmetic and copies ran while one was open for 0% of the time, Pallas kernels for 0%

profile of v1, /device:TPU:0, one launch (start us, length us, event | category | flops | bytes accessed | tf_op | source)
XLA Modules:
  0.0 252.7 jit_solution(15622702031539780455)
XLA Ops:
  6.5 0.0 all-gather.2.cloned.1.call-start
  6.5 0.8 copy.9
  7.3 0.8 copy.10
  8.1 0.9 convert_element_type.9
  9.0 0.1 select_reduce_fusion
  9.1 0.8 pad_maximum_fusion
  9.9 0.0 all-gather.2.cloned.1.call-update
  9.9 0.0 reduce-scatter.2.cloned.1.call-start
  10.0 76.9 %all-gather.2.cloned.1.call-done = f32[512,3600]{1,0:T(8,128)} async-done(((f32[16,3600]{1,0:T(8,128)}), f32[512,3600]{1,0:T(8,128)}) %all-gather.2.cloned.1.call-update) | async-done | bytes 7372816 | tf_op jit(solution)/shard_map/all_gather | solution.py:17
  86.9 1.1 fusion.22
  88.0 6.3 %fusion.2 = f32[512,512]{1,0:T(8,128)S(1)} fusion(f32[512,3600]{1,0:T(8,128)} %all-gather.2.cloned.1.call-done, bf16[1,3584,512]{2,1,0:T(8,128)(2,1)} %param.9), kind=kOutput, calls=%fused_computation.3 | convolution fusion | flops 1879048192 | bytes 8388608 | tf_op jit(solution)/shard_map/dot_general | solution.py:21
  94.3 11.3 %multiply_convert_fusion = bf16[512,3584]{1,0:T(8,128)(2,1)} fusion(bf16[1,512,3584]{2,1,0:T(8,128)(2,1)} %param.11, f32[512]{0:T(512)S(1)} %fusion.22, bf16[1,3584,512]{2,1,0:T(8,128)(2,1)} %param.10, f32[512,3600]{1,0:T(8,128)} %all-gather.2.cloned.1.call-done, f32[512,512]{1,0:T(8,128)S(1)} %fusion.2), kind=kOutput, calls=%fused_computation | convolution fusion | flops 3763339264 | bytes 15730688 | tf_op jit(solution)/shard_map/dot_general | solution.py:24
  105.7 0.0 reduce-scatter.2.cloned.1.call-update
  105.7 140.2 %reduce-scatter.2.cloned.1.call-done = bf16[16,3584]{1,0:T(8,128)(2,1)} async-done(((bf16[512,3584]{1,0:T(8,128)(2,1)}), bf16[16,3584]{1,0:T(8,128)(2,1)}) %reduce-scatter.2.cloned.1.call-update) | async-done | bytes 114704 | tf_op jit(solution)/shard_map/reduce_scatter | solution.py:28
  (1 shorter events, 0.0 us)
Async XLA Ops:
  6.5 80.4 %all-gather.2.cloned.1.call-start = ((), (), s32[]{:S(2)}) async-start(), calls=%async_computation.1 | async-start | bytes 7839744 | tf_op jit(solution)/shard_map/all_gather | solution.py:17
  9.9 235.9 %reduce-scatter.2.cloned.1.call-start = ((), (), s32[]{:S(2)}) async-start(), calls=%async_computation.2 | async-start | bytes 3784704 | tf_op jit(solution)/shard_map/reduce_scatter | solution.py:28
Sparse Core Ops, SparseCore 0:
  10.2 76.6 all-gather.1
  105.8 140.0 reduce-scatter.1
